TPU v7x, 32 devices: a whole 2x2x4 slice. The times are simulated.
32 devices in a mesh: tp: 8 (over y, x, core), dp: 4 (over z).
Axes of the slice: x: 2, y: 2, z: 4, core: 2. Of those that a mesh axis runs over, the one named last changes fastest.
Arguments:
- activations: bfloat16 [64, 512, 4096], P('dp', None, 'tp'), may hold values from -6 to 6
- query_output_cotangent: bfloat16 [64, 512, 4096], P('dp', None, 'tp'), may hold values from -6 to 6
- value_output_cotangent: bfloat16 [64, 512, 4096], P('dp', None, 'tp'), may hold values from -6 to 6
- lengths: int32 [64], P('dp'), may hold values from 1 to 512
- reducing_matrices_pair: bfloat16 [2, 4096, 128], P(None, 'tp'), may hold values from -0.09375 to 0.09375
- expanding_matrices_pair: bfloat16 [2, 128, 4096], P(None, None, 'tp'), may hold values from -0.5 to 0.5
- width_side_projections: bfloat16 [2, 4096, 128], P(None, 'tp'), may hold values from -0.09375 to 0.09375
- narrow_random_sketch: bfloat16 [128, 16], replicated, may hold values from -0.5 to 0.5
- projected_first_moment: float32 [8192], replicated, may hold values from -6 to 6
- projected_second_moment: float32 [8192], replicated, may hold values from 0.1 to 10
- targets: bfloat16 [1024, 8192], P('dp', 'tp'), may hold values from -6 to 6
Outputs:
- scores: float32 [64, 1024], P('dp', 'tp')
All inputs are finite; a program needn't handle non-finite values.
Results may differ from a plain program's by a relative error of at most 0.023.
Values may be sent and summed in bfloat16 or wider, within the bound.
A program may use at most 128 MiB of HBM per device.

v0:
```python
import math
import jax
import jax.numpy as jnp
from jax import lax
from jax.sharding import PartitionSpec as P


def compute_features(token_sums, token_mask, layout, rank_cols):
    wide_cols = (token_sums.shape[-1] - 4 * rank_cols) // 3
    bounds = [
        0,
        rank_cols,
        2 * rank_cols,
        2 * rank_cols + wide_cols,
        3 * rank_cols + wide_cols,
        3 * rank_cols + 2 * wide_cols,
        4 * rank_cols + 2 * wide_cols,
        4 * rank_cols + 3 * wide_cols,
    ]
    pieces = [token_sums[..., bounds[i] : bounds[i + 1]] for i in range(7)]
    down_q, down_v, input_side, back_q, output_q, back_v, output_v = pieces
    weights = token_mask[..., None]
    pattern = layout + "r," + layout + "k->erk"

    def outer_sum(left_side, right_side):
        return jnp.einsum(pattern, left_side, right_side, precision=lax.Precision.HIGHEST)

    stacked = jnp.stack(
        [
            outer_sum(back_q * weights, input_side),
            outer_sum(back_v * weights, input_side),
            outer_sum(down_q * weights, output_q),
            outer_sum(down_v * weights, output_v),
        ],
        axis=1,
    )
    return stacked.reshape(stacked.shape[0], -1)


def adam_update(features, first_moment, second_moment):
    mixed = 0.9 * first_moment + 0.1 * features
    spread = 0.999 * second_moment + 0.001 * features * features
    return mixed / (jnp.sqrt(spread) + 1e-08)


def combine_factors(reducing_matrices_pair, expanding_matrices_pair, narrow_random_sketch):
    attention_key_reducer = jnp.dot(
        reducing_matrices_pair[0], narrow_random_sketch, preferred_element_type=jnp.float32
    ).astype(jnp.bfloat16)
    value_down_factor = jnp.dot(
        reducing_matrices_pair[1], narrow_random_sketch, preferred_element_type=jnp.float32
    ).astype(jnp.bfloat16)
    query_up_factor = jnp.dot(
        expanding_matrices_pair[0].T, narrow_random_sketch, preferred_element_type=jnp.float32
    ).astype(jnp.bfloat16)
    value_up_factor = jnp.dot(
        expanding_matrices_pair[1].T, narrow_random_sketch, preferred_element_type=jnp.float32
    ).astype(jnp.bfloat16)
    return (attention_key_reducer, value_down_factor, query_up_factor, value_up_factor)


def body(
    activations,
    query_output_cotangent,
    value_output_cotangent,
    lengths,
    reducing_matrices_pair,
    expanding_matrices_pair,
    width_side_projections,
    narrow_random_sketch,
    projected_first_moment,
    projected_second_moment,
    targets,
):
    attention_key_reducer, value_down_factor, query_up_factor, value_up_factor = combine_factors(
        reducing_matrices_pair, expanding_matrices_pair, narrow_random_sketch
    )
    rank_cols = narrow_random_sketch.shape[1]
    w_left = jnp.concatenate(
        [attention_key_reducer, value_down_factor, width_side_projections[0]], axis=1
    )
    w_query = jnp.concatenate([query_up_factor, width_side_projections[1]], axis=1)
    w_value = jnp.concatenate([value_up_factor, width_side_projections[1]], axis=1)
    groups = lax.axis_size("tp")
    member = lax.axis_index("tp")
    local_ex = activations.shape[0]
    seq_len = activations.shape[1]
    feature_count = projected_first_moment.shape[0]
    positions = jnp.arange(seq_len, dtype=jnp.int32)
    token_mask = (positions[None, :] < lengths[:, None]).astype(jnp.float32)
    target_float = targets.astype(jnp.float32)
    target_sq = jnp.sum(target_float * target_float, axis=1)
    own_rows = local_ex // groups
    left_part = jnp.einsum("esd,dc->esc", activations, w_left, preferred_element_type=jnp.float32)
    right_q = jnp.einsum(
        "esd,dc->esc", query_output_cotangent, w_query, preferred_element_type=jnp.float32
    )
    right_v = jnp.einsum(
        "esd,dc->esc", value_output_cotangent, w_value, preferred_element_type=jnp.float32
    )
    token_sums = lax.psum_scatter(
        jnp.concatenate([left_part, right_q, right_v], axis=-1).astype(jnp.bfloat16),
        "tp",
        scatter_dimension=0,
        tiled=True,
    ).astype(jnp.float32)
    own_mask = lax.dynamic_slice_in_dim(token_mask, member * own_rows, own_rows, 0)
    features = compute_features(token_sums, own_mask, "es", rank_cols)
    update = adam_update(features, projected_first_moment, projected_second_moment)
    squares = jnp.sum(update * update, axis=1)
    target_total = lax.psum(target_sq, "tp")
    own_train = (update * lax.rsqrt(squares + 1e-06)[:, None]).astype(jnp.bfloat16)
    train_rows = lax.all_to_all(own_train, "tp", split_axis=1, concat_axis=0, tiled=True)
    unit_targets = (target_float * lax.rsqrt(target_total + 1e-06)[:, None]).astype(jnp.bfloat16)
    partial_scores = lax.dot_general(
        train_rows,
        lax.all_gather(unit_targets, "dp", axis=0, tiled=True),
        (((1,), (1,)), ((), ())),
        preferred_element_type=jnp.float32,
    )
    scores = lax.psum_scatter(
        partial_scores.astype(jnp.bfloat16), "tp", scatter_dimension=1, tiled=True
    ).astype(jnp.float32)
    return scores * math.sqrt(feature_count)


def solution(mesh):
    placed = (
        P("dp", None, "tp"),
        P("dp", None, "tp"),
        P("dp", None, "tp"),
        P("dp"),
        P(None, "tp", None),
        P(None, None, "tp"),
        P(None, "tp", None),
        P(),
        P(),
        P(),
        P("dp", "tp"),
    )
    return jax.shard_map(body, mesh=mesh, in_specs=placed, out_specs=P("dp", "tp"), check_vma=False)
```

profile of v0, /device:TPU:0, one launch (start us, length us, event | category | flops | bytes accessed | tf_op | source)
XLA Modules:
  0.0 158.5 jit_solution(14947241364090054816)
XLA Ops:
  7.4 0.7 copy-done
  8.1 1.0 convolution_convert_fusion.1
  9.1 1.0 convolution_convert_fusion.2
  10.1 1.0 convolution_convert_fusion.3
  11.2 1.1 convolution_convert_fusion.4
  12.2 1.0 fusion.41
  13.5 6.4 %convert_bitcast_fusion.1 = bf16[16,512,144]{1,2,0:T(8,128)(2,1)S(1)} fusion(bf16[16,512,512]{2,1,0:T(8,128)(2,1)} %param.13, bf16[512,16]{0,1:T(8,128)(2,1)S(1)} %convolution_convert_fusion.1, bf16[512,128]{0,1:T(8,128)(2,1)S(1)} %bitcast.53), kind=kOutput, calls=%fused_computation.2 | convolution fusion | flops 1209434112 | bytes 10895360 | tf_op jit(solution)/shard_map/esd,dc->esc/dot_general | solution.py:98
  19.9 2.9 %convert_bitcast_fusion.2 = bf16[16,512,144]{1,2,0:T(8,128)(2,1)S(1)} fusion(bf16[16,512,512]{2,1,0:T(8,128)(2,1)S(1)} %copy-done.1, bf16[512,16]{0,1:T(8,128)(2,1)S(1)} %convolution_convert_fusion.2, bf16[512,128]{0,1:T(8,128)(2,1)S(1)} %bitcast.54), kind=kOutput, calls=%fused_computation.3 | convolution fusion | flops 1209434112 | bytes 10895360 | tf_op jit(solution)/shard_map/esd,dc->esc/dot_general | solution.py:95
  23.3 2.9 %convert_bitcast_fusion = bf16[16,512,160]{1,2,0:T(8,128)(2,1)S(1)} fusion(bf16[16,512,512]{2,1,0:T(8,128)(2,1)S(1)} %copy-done.2, bf16[512,128]{0,1:T(8,128)(2,1)S(1)} %bitcast.56, bf16[512,16]{0,1:T(8,128)(2,1)S(1)} %convolution_convert_fusion.3, bf16[512,16]{0,1:T(8,128)(2,1)S(1)} %convolution_convert_fusion.4), kind=kOutput, calls=%fused_computation.1 | convolution fusion | flops 1343979520 | bytes 11173888 | tf_op jit(solution)/shard_map/esd,dc->esc/dot_general | solution.py:94
  26.2 3.4 %pad_maximum_fusion = bf16[16,512,448]{1,2,0:T(8,128)(2,1)} fusion(bf16[16,512,144]{1,2,0:T(8,128)(2,1)S(1)} %convert_bitcast_fusion.1, bf16[16,512,144]{1,2,0:T(8,128)(2,1)S(1)} %convert_bitcast_fusion.2, bf16[16,512,160]{1,2,0:T(8,128)(2,1)S(1)} %convert_bitcast_fusion), kind=kLoop, calls=%fused_computation | loop fusion | flops 22020096 | bytes 14680064 | tf_op jit(solution)/shard_map/concatenate | solution.py:102
  29.6 1.0 copy-done.3
  30.7 15.1 %psum.7 = f32[256]{0:T(256)S(1)} all-reduce(f32[256]{0:T(256)S(1)} %fusion), channel_id=1, replica_groups=mesh['tp'=8,'dp'=4] {'tp'}, use_global_device_ids=true, to_apply=%region_3.0 | all-reduce | flops 256 | bytes 2048 | tf_op jit(solution)/shard_map/psum | solution.py:111
  45.9 1.0 fusion.1
  47.2 52.2 %reduce-scatter.5.cloned.1.call-done = bf16[2,512,448]{1,2,0:T(8,128)(2,1)} async-done(((bf16[16,512,448]{1,2,0:T(8,128)(2,1)}), bf16[2,512,448]{1,2,0:T(8,128)(2,1)}) %reduce-scatter.5.cloned.1.call-update) | async-done | bytes 917520 | tf_op jit(solution)/shard_map/reduce_scatter | solution.py:101
  99.3 1.4 convert_element_type.39
  100.8 1.3 convolution_bitcast_fusion.3
  102.0 1.3 convolution_bitcast_fusion.2
  103.3 1.3 convolution_bitcast_fusion.1
  104.6 1.3 convolution_bitcast_fusion
  106.2 7.4 %all_to_all.16 = bf16[2,8,1024]{2,0,1:T(2,128)(2,1)S(1)} all-to-all(bf16[2,8,1024]{2,0,1:T(2,128)(2,1)S(1)} %copy.33), channel_id=1, replica_groups=mesh['tp'=8,'dp'=4] {'tp'}, dimensions={1} | all-to-all | bytes 65536 | tf_op jit(solution)/shard_map/all_to_all | solution.py:113
  113.6 2.2 %convolution_convert_fusion = bf16[16,1024]{1,0:T(8,128)(2,1)S(1)} fusion(bf16[16,1024]{1,0:T(8,128)(2,1)S(1)} %all_to_all.14, bf16[1024,1024]{1,0:T(8,128)(2,1)} %all-gather.2.cloned.1.call-done), kind=kOutput, calls=%fused_computation.6 | convolution fusion | flops 33570816 | bytes 2162688 | tf_op jit(solution)/shard_map/dot_general | solution.py:115
  115.8 0.8 copy.38
  116.7 32.9 %reduce-scatter.7.cloned.1.call-done = bf16[128,16]{1,0:T(8,128)(2,1)} async-done(((bf16[1024,16]{1,0:T(8,128)(2,1)}), bf16[128,16]{1,0:T(8,128)(2,1)}) %reduce-scatter.7.cloned.1.call-update) | async-done | bytes 4112
  149.6 0.8 copy.39
  (37 shorter events, 2.2 us)
Async XLA Ops:
  7.4 0.7 copy-start
  7.4 92.0 %reduce-scatter.5.cloned.1.call-start = ((), (), s32[]{:S(2)}) async-start(), calls=%async_computation.3 | async-start | bytes 8257536 | tf_op jit(solution)/shard_map/reduce_scatter | solution.py:101
  13.5 6.4 %copy-start.1 = (bf16[16,512,512]{2,1,0:T(8,128)(2,1)S(1)}, bf16[16,512,512]{2,1,0:T(8,128)(2,1)}, u32[]{:S(2)}) copy-start(bf16[16,512,512]{2,1,0:T(8,128)(2,1)} %param.12) | copy-start | bytes 25165828
  19.9 3.4 %copy-start.2 = (bf16[16,512,512]{2,1,0:T(8,128)(2,1)S(1)}, bf16[16,512,512]{2,1,0:T(8,128)(2,1)}, u32[]{:S(2)}) copy-start(bf16[16,512,512]{2,1,0:T(8,128)(2,1)} %param.11) | copy-start | bytes 25165828
  29.5 1.0 copy-start.3
  29.5 17.4 %copy-start.4 = (f32[8192]{0:T(1024)S(1)}, f32[8192]{0:T(1024)}, u32[]{:S(2)}) copy-start(f32[8192]{0:T(1024)} %param.19) | copy-start | bytes 98308
  29.5 17.4 %copy-start.5 = (f32[8192]{0:T(1024)S(1)}, f32[8192]{0:T(1024)}, u32[]{:S(2)}) copy-start(f32[8192]{0:T(1024)} %param.20) | copy-start | bytes 98308
  29.5 17.5 %copy-start.6 = (s32[16]{0:T(128)S(1)}, s32[16]{0:T(128)}, u32[]{:S(2)}) copy-start(s32[16]{0:T(128)} %param.14) | copy-start | bytes 196
  29.6 84.0 %all-gather.2.cloned.1.call-start = ((), (), s32[]{:S(2)}) async-start(), calls=%async_computation.4 | async-start | bytes 2621440 | tf_op jit(solution)/shard_map/all_gather | solution.py:117
  46.9 102.7 %reduce-scatter.7.cloned.1.call-start = ((), (), s32[]{:S(2)}) async-start(), calls=%async_computation.5 | async-start | bytes 294912
Sparse Core Ops, SparseCore 0:
  29.7 69.6 reduce-scatter.4
  116.8 32.7 reduce-scatter.6
Sparse Core Ops, SparseCore 1:
  47.0 44.9 all-gather.1
where the time goes:
time: 159 us; the launch traced here: 158 us
  waiting for transfers between devices  85.1 us (54%)
  matrix products  23.6 us (15%)
  blocking collectives  22.5 us (14%)
  between operations  15 us (9%)
  other arithmetic  6.89 us (4%)
  local copies, waits for them, and re-layouts  5.24 us (3%)
    reduce_scatter x1, waiting for transfers between devices, body(): lax.psum_scatter(jnp.concatenate([left_part, right_q, right_v], axis=-1)....  52.2 us
    unnamed x4, waiting for transfers between devices  32.9 us
    psum x1, blocking collectives, body(): target_total = lax.psum(target_sq, 'tp')  15.1 us
    all_to_all x1, blocking collectives, body(): lax.all_to_all(own_train, 'tp', split_axis=1, concat_axis=0, tiled=True)  7.37 us
    dot_general x1, matrix products, body(): jnp.einsum('esd,dc->esc', value_output_cotangent, w_value, preferred_elem...  6.4 us
    dot_general x4, matrix products, outer_sum(): jnp.einsum(pattern, left_side, right_side, precision=lax.Precision.HIGHEST)  5.09 us
    unnamed x18, local copies, waits for them, and re-layouts  4.05 us
    concatenate x1, other arithmetic, body(): jnp.concatenate([left_part, right_q, right_v], axis=-1).astype(jnp.bfloat16)  3.35 us
  transfers between devices with their start and end apart: 3, of which 2 were waited for; matrix products, arithmetic and copies ran while one was open for 5% of the time, Pallas kernels for 0%

commit v1 on v0

--- a/solution.py
+++ b/solution.py
@@ -108,7 +108,13 @@
     features = compute_features(token_sums, own_mask, "es", rank_cols)
     update = adam_update(features, projected_first_moment, projected_second_moment)
     squares = jnp.sum(update * update, axis=1)
-    target_total = lax.psum(target_sq, "tp")
+    size = lax.axis_size("tp")
+    target_total, reach = (target_sq, 1)
+    while reach < size:
+        target_total = target_total + lax.ppermute(
+            target_total, "tp", [(i_2, i_2 ^ reach) for i_2 in range(size)]
+        )
+        reach = 2 * reach
     own_train = (update * lax.rsqrt(squares + 1e-06)[:, None]).astype(jnp.bfloat16)
     train_rows = lax.all_to_all(own_train, "tp", split_axis=1, concat_axis=0, tiled=True)
     unit_targets = (target_float * lax.rsqrt(target_total + 1e-06)[:, None]).astype(jnp.bfloat16)

time: 159 us -> 159 us (level)
  blocking collectives: 22.5 us -> 7.37 us
  waiting for transfers between devices: 85.1 us -> 94.9 us
  starting transfers between devices: 0.09 us -> 5.46 us
    psum x1 -> x0, blocking collectives: 15.1 us -> none  [body(): target_total = lax.psum(target_sq, 'tp')]
    reduce_scatter x1, waiting for transfers between devices: 52.2 us -> 58 us  [body(): lax.psum_scatter(jnp.concatenate([left_part, right_q, right_v], axis=-1)....]
    ppermute x0 -> x3, starting transfers between devices: none -> 5.37 us  [body(): lax.ppermute(target_total, 'tp', [(i_2, i_2 ^ reach) for i_2 in range(siz...]
    ppermute x0 -> x3, waiting for transfers between devices: none -> 3.91 us  [body(): lax.ppermute(target_total, 'tp', [(i_2, i_2 ^ reach) for i_2 in range(siz...]
  transfers between devices with their start and end apart: 3 -> 6, of which waited for: 2 -> 5; matrix products, arithmetic and copies ran while one was open for 5% -> 5% of each run, Pallas kernels for 0% -> 0%
where the time goes in v1:
time: 159 us; the launch traced here: 158 us
  waiting for transfers between devices  94.9 us (60%)
  matrix products  23.6 us (15%)
  between operations  15 us (9%)
  blocking collectives  7.37 us (5%)
  other arithmetic  6.87 us (4%)
  starting transfers between devices  5.46 us (3%)
  local copies, waits for them, and re-layouts  5.25 us (3%)
    reduce_scatter x1, waiting for transfers between devices, body(): lax.psum_scatter(jnp.concatenate([left_part, right_q, right_v], axis=-1)....  58 us
    unnamed x4, waiting for transfers between devices  32.9 us
    all_to_all x1, blocking collectives, body(): lax.all_to_all(own_train, 'tp', split_axis=1, concat_axis=0, tiled=True)  7.37 us
    dot_general x1, matrix products, body(): jnp.einsum('esd,dc->esc', value_output_cotangent, w_value, preferred_elem...  6.4 us
    ppermute x3, starting transfers between devices, body(): lax.ppermute(target_total, 'tp', [(i_2, i_2 ^ reach) for i_2 in range(siz...  5.37 us
    dot_general x4, matrix products, outer_sum(): jnp.einsum(pattern, left_side, right_side, precision=lax.Precision.HIGHEST)  5.09 us
    unnamed x18, local copies, waits for them, and re-layouts  4.06 us
    ppermute x3, waiting for transfers between devices, body(): lax.ppermute(target_total, 'tp', [(i_2, i_2 ^ reach) for i_2 in range(siz...  3.91 us
  transfers between devices with their start and end apart: 6, of which 5 were waited for; matrix products, arithmetic and copies ran while one was open for 5% of the time, Pallas kernels for 0%

profile of v1, /device:TPU:0, one launch (start us, length us, event | category | flops | bytes accessed | tf_op | source)
XLA Modules:
  0.0 158.5 jit_solution(494498293146888636)
XLA Ops:
  8.1 1.0 convolution_convert_fusion.1
  9.1 1.0 convolution_convert_fusion.2
  10.1 1.0 convolution_convert_fusion.3
  11.2 1.1 convolution_convert_fusion.4
  12.2 1.0 fusion.41
  13.5 6.4 %convert_bitcast_fusion.1 = bf16[16,512,144]{1,2,0:T(8,128)(2,1)S(1)} fusion(bf16[16,512,512]{2,1,0:T(8,128)(2,1)} %param.13, bf16[512,16]{0,1:T(8,128)(2,1)S(1)} %convolution_convert_fusion.1, bf16[512,128]{0,1:T(8,128)(2,1)S(1)} %bitcast.53), kind=kOutput, calls=%fused_computation.2 | convolution fusion | flops 1209434112 | bytes 10895360 | tf_op jit(solution)/shard_map/esd,dc->esc/dot_general | solution.py:98
  19.9 2.9 %convert_bitcast_fusion.2 = bf16[16,512,144]{1,2,0:T(8,128)(2,1)S(1)} fusion(bf16[16,512,512]{2,1,0:T(8,128)(2,1)S(1)} %copy-done.1, bf16[512,16]{0,1:T(8,128)(2,1)S(1)} %convolution_convert_fusion.2, bf16[512,128]{0,1:T(8,128)(2,1)S(1)} %bitcast.54), kind=kOutput, calls=%fused_computation.3 | convolution fusion | flops 1209434112 | bytes 10895360 | tf_op jit(solution)/shard_map/esd,dc->esc/dot_general | solution.py:95
  23.3 2.9 %convert_bitcast_fusion = bf16[16,512,160]{1,2,0:T(8,128)(2,1)S(1)} fusion(bf16[16,512,512]{2,1,0:T(8,128)(2,1)S(1)} %copy-done.2, bf16[512,128]{0,1:T(8,128)(2,1)S(1)} %bitcast.56, bf16[512,16]{0,1:T(8,128)(2,1)S(1)} %convolution_convert_fusion.3, bf16[512,16]{0,1:T(8,128)(2,1)S(1)} %convolution_convert_fusion.4), kind=kOutput, calls=%fused_computation.1 | convolution fusion | flops 1343979520 | bytes 11173888 | tf_op jit(solution)/shard_map/esd,dc->esc/dot_general | solution.py:94
  26.2 3.3 %pad_maximum_fusion = bf16[16,512,448]{1,2,0:T(8,128)(2,1)} fusion(bf16[16,512,144]{1,2,0:T(8,128)(2,1)S(1)} %convert_bitcast_fusion.1, bf16[16,512,144]{1,2,0:T(8,128)(2,1)S(1)} %convert_bitcast_fusion.2, bf16[16,512,160]{1,2,0:T(8,128)(2,1)S(1)} %convert_bitcast_fusion), kind=kLoop, calls=%fused_computation | loop fusion | flops 22020096 | bytes 14680064 | tf_op jit(solution)/shard_map/concatenate | solution.py:102
  29.6 1.0 copy-done.3
  32.1 2.8 %collective-permute-start.1 = (f32[256]{0:T(256)S(1)}, f32[256]{0:T(256)S(1)}, u32[]{:S(2)}, u32[]{:S(2)}) collective-permute-start(f32[256]{0:T(256)S(1)} %add.95), channel_id=1, source_target_pairs={{0,8},{4,12},{8,0},{12,4},{16,24},{20,28},{24,16},{28,20},{1,9},{5... | collective-permute-start | bytes 3080 | tf_op jit(solution)/shard_map/ppermute | solution.py:114
  34.9 1.5 collective-permute-done.1
  36.4 2.1 %collective-permute-start.2 = (f32[256]{0:T(256)S(1)}, f32[256]{0:T(256)S(1)}, u32[]{:S(2)}, u32[]{:S(2)}) collective-permute-start(f32[256]{0:T(256)S(1)} %add.96), channel_id=1, source_target_pairs={{0,16},{4,20},{8,24},{12,28},{16,0},{20,4},{24,8},{28,12},{1,17},{... | collective-permute-start | bytes 3080 | tf_op jit(solution)/shard_map/ppermute | solution.py:114
  38.5 1.5 collective-permute-done.2
  40.0 1.0 fusion.1
  41.3 58.0 %reduce-scatter.5.cloned.1.call-done = bf16[2,512,448]{1,2,0:T(8,128)(2,1)} async-done(((bf16[16,512,448]{1,2,0:T(8,128)(2,1)}), bf16[2,512,448]{1,2,0:T(8,128)(2,1)}) %reduce-scatter.5.cloned.1.call-update) | async-done | bytes 917520 | tf_op jit(solution)/shard_map/reduce_scatter | solution.py:101
  99.4 1.4 convert_element_type.39
  100.8 1.3 convolution_bitcast_fusion.3
  102.1 1.3 convolution_bitcast_fusion.2
  103.3 1.3 convolution_bitcast_fusion.1
  104.6 1.3 convolution_bitcast_fusion
  106.2 7.4 %all_to_all.16 = bf16[2,8,1024]{2,0,1:T(2,128)(2,1)S(1)} all-to-all(bf16[2,8,1024]{2,0,1:T(2,128)(2,1)S(1)} %copy.33), channel_id=1, replica_groups=mesh['tp'=8,'dp'=4] {'tp'}, dimensions={1} | all-to-all | bytes 65536 | tf_op jit(solution)/shard_map/all_to_all | solution.py:119
  113.6 2.2 %convolution_convert_fusion = bf16[16,1024]{1,0:T(8,128)(2,1)S(1)} fusion(bf16[16,1024]{1,0:T(8,128)(2,1)S(1)} %all_to_all.14, bf16[1024,1024]{1,0:T(8,128)(2,1)} %all-gather.2.cloned.1.call-done), kind=kOutput, calls=%fused_computation.6 | convolution fusion | flops 33570816 | bytes 2162688 | tf_op jit(solution)/shard_map/dot_general | solution.py:121
  116.7 32.9 %reduce-scatter.7.cloned.1.call-done = bf16[128,16]{1,0:T(8,128)(2,1)} async-done(((bf16[1024,16]{1,0:T(8,128)(2,1)}), bf16[128,16]{1,0:T(8,128)(2,1)}) %reduce-scatter.7.cloned.1.call-update) | async-done | bytes 4112
  (44 shorter events, 5.9 us)
Async XLA Ops:
  7.4 0.7 copy-start
  7.4 92.0 %reduce-scatter.5.cloned.1.call-start = ((), (), s32[]{:S(2)}) async-start(), calls=%async_computation.3 | async-start | bytes 8257536 | tf_op jit(solution)/shard_map/reduce_scatter | solution.py:101
  13.5 6.4 %copy-start.1 = (bf16[16,512,512]{2,1,0:T(8,128)(2,1)S(1)}, bf16[16,512,512]{2,1,0:T(8,128)(2,1)}, u32[]{:S(2)}) copy-start(bf16[16,512,512]{2,1,0:T(8,128)(2,1)} %param.12) | copy-start | bytes 25165828
  19.9 3.4 %copy-start.2 = (bf16[16,512,512]{2,1,0:T(8,128)(2,1)S(1)}, bf16[16,512,512]{2,1,0:T(8,128)(2,1)}, u32[]{:S(2)}) copy-start(bf16[16,512,512]{2,1,0:T(8,128)(2,1)} %param.11) | copy-start | bytes 25165828
  29.5 1.0 copy-start.3
  29.5 11.6 %copy-start.4 = (f32[8192]{0:T(1024)S(1)}, f32[8192]{0:T(1024)}, u32[]{:S(2)}) copy-start(f32[8192]{0:T(1024)} %param.19) | copy-start | bytes 98308
  29.5 11.6 %copy-start.5 = (f32[8192]{0:T(1024)S(1)}, f32[8192]{0:T(1024)}, u32[]{:S(2)}) copy-start(f32[8192]{0:T(1024)} %param.20) | copy-start | bytes 98308
  29.5 11.7 %copy-start.6 = (s32[16]{0:T(128)S(1)}, s32[16]{0:T(128)}, u32[]{:S(2)}) copy-start(s32[16]{0:T(128)} %param.14) | copy-start | bytes 196
  29.5 84.1 %all-gather.2.cloned.1.call-start = ((), (), s32[]{:S(2)}) async-start(), calls=%async_computation.4 | async-start | bytes 2621440 | tf_op jit(solution)/shard_map/all_gather | solution.py:123
  30.7 1.3 collective-permute-start
  32.1 4.4 %collective-permute-start.1 = (f32[256]{0:T(256)S(1)}, f32[256]{0:T(256)S(1)}, u32[]{:S(2)}, u32[]{:S(2)}) collective-permute-start(f32[256]{0:T(256)S(1)} %add.95), channel_id=1, source_target_pairs={{0,8},{4,12},{8,0},{12,4},{16,24},{20,28},{24,16},{28,20},{1,9},{5... | collective-permute-start | bytes 3080 | tf_op jit(solution)/shard_map/ppermute | solution.py:114
  36.4 3.6 %collective-permute-start.2 = (f32[256]{0:T(256)S(1)}, f32[256]{0:T(256)S(1)}, u32[]{:S(2)}, u32[]{:S(2)}) collective-permute-start(f32[256]{0:T(256)S(1)} %add.96), channel_id=1, source_target_pairs={{0,16},{4,20},{8,24},{12,28},{16,0},{20,4},{24,8},{28,12},{1,17},{... | collective-permute-start | bytes 3080 | tf_op jit(solution)/shard_map/ppermute | solution.py:114
  41.0 108.6 %reduce-scatter.7.cloned.1.call-start = ((), (), s32[]{:S(2)}) async-start(), calls=%async_computation.5 | async-start | bytes 294912
Sparse Core Ops, SparseCore 0:
  29.7 69.6 reduce-scatter.4
  116.9 32.6 reduce-scatter.6
Sparse Core Ops, SparseCore 1:
  41.1 47.3 all-gather.1
